TPU v7x, 32 devices: a whole 2x2x4 slice. The times are simulated.
32 devices in a mesh: tm: 4 (over y, x), space: 8 (over z, core).
Axes of the slice: x: 2, y: 2, z: 4, core: 2. Of those that a mesh axis runs over, the one named last changes fastest.
Arguments:
- starts: float32 [4, 3, 64, 64, 128], P('tm', None, 'space'), may hold values from -6 to 6
- strain: bfloat16 [4, 9, 64, 64, 128], P('tm', None, 'space'), may hold values from -0.59765625 to 0.59765625
Outputs:
- corrected: float32 [4, 3, 64, 64, 128], P('tm', None, 'space')
All inputs are finite; a program needn't handle non-finite values.
Results may differ from a plain program's by a relative error of at most 0.0003.
Values sent between devices are 32-bit elements; how exact they have to be, the bound alone decides.
A program may use at most 128 MiB of HBM per device.

v0:
```python
import jax
import jax.numpy as jnp
from jax import lax
from jax.sharding import PartitionSpec as P

COARSEN = 4


kernel_near = 0.8
kernel_far = 0.2
diffusion = 0.08
coarse_rate = 0.1


def padded_2(cells, sides, width):
    for axis, dim in sides:
        count = lax.axis_size(axis)
        ends = count - 1
        head = lax.slice_in_dim(cells, 0, width, axis=dim)
        tail = lax.slice_in_dim(cells, cells.shape[dim] - width, cells.shape[dim], axis=dim)
        cells = jnp.concatenate(
            [
                lax.ppermute(tail, axis, [(i, (i + 1) % count) for i in range(ends)]),
                cells,
                lax.ppermute(head, axis, [((i + 1) % count, i) for i in range(ends)]),
            ],
            axis=dim,
        )
    return cells


def passed_along(block, axis, distance):
    devices = range(lax.axis_size(axis))
    route = [(i - distance, i) for i in devices if i - distance in devices]
    return lax.ppermute(block, axis, route)


def depth_terms(padded, field, depth):
    near_sum = padded[:, 3 : 3 + depth] + padded[:, 1 : 1 + depth] - 2.0 * field
    far_sum = padded[:, 4 : 4 + depth] + padded[:, 0:depth] - 2.0 * field
    return kernel_near * near_sum + kernel_far * far_sum


def plane_terms(field):
    total = jnp.zeros_like(field)
    for along in (2, 3):
        near_sum = jnp.roll(field, 1, along) + jnp.roll(field, -1, along) - 2.0 * field
        far_sum = jnp.roll(field, 2, along) + jnp.roll(field, -2, along) - 2.0 * field
        total = total + kernel_near * near_sum + kernel_far * far_sum
    return total


def stretch_terms(field, strain):
    result = []
    for row in range(3):
        acc = strain[3 * row].astype(jnp.float32) * field[0]
        acc = acc + strain[3 * row + 1].astype(jnp.float32) * field[1]
        acc = acc + strain[3 * row + 2].astype(jnp.float32) * field[2]
        result.append(acc)
    return jnp.stack(result, axis=0)


def restrict_field(field):
    comps, depth, width_x, width_y = field.shape
    blocks = field.reshape(
        comps, depth // COARSEN, COARSEN, width_x // COARSEN, COARSEN, width_y // COARSEN, COARSEN
    )
    return jnp.mean(blocks, axis=(2, 4, 6))


def prolong_field(coarse):
    comps, depth, width_x, width_y = coarse.shape
    spread = jnp.broadcast_to(
        coarse[:, :, None, :, None, :, None],
        (comps, depth, COARSEN, width_x, COARSEN, width_y, COARSEN),
    )
    return spread.reshape(comps, depth * COARSEN, width_x * COARSEN, width_y * COARSEN)


def coarse_step(field, padded):
    near_sum = padded[..., 2:, :, :] + padded[..., :-2, :, :]
    near_sum = near_sum + jnp.roll(field, 1, -2) + jnp.roll(field, -1, -2)
    near_sum = near_sum + jnp.roll(field, 1, -1) + jnp.roll(field, -1, -1)
    return field + coarse_rate * (near_sum - 6.0 * field)


def coarse_apply(field):
    padded = padded_2(field, (("space", 1),), 1)
    return coarse_step(field, padded)


def solve_small(factor, vector):
    lower = lax.linalg.triangular_solve(factor, vector[:, None], left_side=True, lower=True)
    upper = lax.linalg.triangular_solve(factor, lower, left_side=True, lower=True, transpose_a=True)
    return upper[:, 0]


def local(starts, strain):
    field = starts[0]
    depth = field.shape[1]
    padded = padded_2(field, (("space", 1),), 2)
    depth_part = depth_terms(padded, field, depth)
    fine_ends = (
        field + stretch_terms(field, strain[0]) + diffusion * (depth_part + plane_terms(field))
    )
    start_coarse = restrict_field(field)
    end_coarse = restrict_field(fine_ends)
    slices = lax.axis_size("tm")
    slice_index = lax.axis_index("tm")
    start_pad = padded_2(start_coarse, (("space", 1),), 1)
    folded = end_coarse - coarse_step(start_coarse, start_pad)
    snap_basis, images = (
        lax.all_gather(start_coarse[None], "tm", axis=0, tiled=True),
        lax.all_gather(folded[None], "tm", axis=0, tiled=True),
    )
    flat_basis = snap_basis.reshape(slices, -1)
    flat_images = images.reshape(slices, -1)
    local_gram = jnp.dot(flat_basis, flat_basis.T, precision=lax.Precision.HIGHEST)
    gram_matrix = lax.psum(local_gram, "space")
    factor = jnp.linalg.cholesky(gram_matrix)
    shape = start_coarse.shape

    def kapply(gap):
        product = jnp.dot(flat_basis, gap.reshape(-1), precision=lax.Precision.HIGHEST)
        coeffs = solve_small(factor, lax.psum(product, "space"))
        spanned = jnp.dot(coeffs, flat_images, precision=lax.Precision.HIGHEST).reshape(shape)
        return spanned + coarse_apply(gap)

    def advance(counter, carried):
        incoming = passed_along(end_coarse + carried, "tm", 1)
        gap = jnp.where(slice_index == 0, jnp.zeros_like(incoming), incoming - start_coarse)
        return kapply(gap)

    carried = lax.fori_loop(0, slices - 1, advance, jnp.zeros(shape, jnp.float32))
    corrected = fine_ends + prolong_field(carried)
    return corrected[None]


def solution(mesh):
    return jax.shard_map(
        local,
        mesh=mesh,
        in_specs=(P("tm", None, "space", None, None), P("tm", None, "space", None, None)),
        out_specs=P("tm", None, "space", None, None),
        check_vma=False,
    )
```

profile of v0, /device:TPU:0, one launch (start us, length us, event | category | flops | bytes accessed | tf_op | source)
XLA Modules:
  0.0 253.8 jit_solution(9710605054824545391)
XLA Ops:
  1.1 1.3 collective-permute-start.3
  2.4 3.8 %collective-permute-start.4 = (f32[3,2,64,128]{3,2,1,0:T(8,128)S(1)}, f32[3,2,64,128]{3,2,1,0:T(8,128)}, u32[]{:S(2)}, u32[]{:S(2)}) collective-permute-start(f32[3,2,64,128]{3,2,1,0:T(8,128)S(1)} %get-tuple-element.173), channel_id=1, source_target_pairs={{0,1},{1,2},{2,3},{3,4},{4,5},{5,6},{6,7},{8,9},{9,10},{10,11},{11... | collective-permute-start | bytes 589832 | tf_op jit(solution)/shard_map/ppermute | solution.py:23
  6.2 28.2 %reshape_squeeze.3 = f32[3,2,4,16,4,32,4]{6,5,4,3,2,1,0:T(8,128)} reshape(f32[1,3,8,64,128]{4,3,2,1,0:T(8,128)} %param.4) | data formatting | bytes 1572864 | tf_op jit(solution)/shard_map/reshape;squeeze | solution.py:65
  34.4 9.6 %reduce_sum.18 = f32[3,2,16,32]{3,2,1,0:T(8,128)S(1)} reduce(f32[3,2,4,16,4,32,4]{6,5,4,3,2,1,0:T(8,128)} %reshape_squeeze.3, f32[]{:T(128)} %constant.87.clone.1), dimensions={2,4,6}, to_apply=%region_1.2 | reduce | flops 193536 | bytes 798724 | tf_op jit(solution)/shard_map/reduce_sum | solution.py:68
  45.9 5.2 %collective-permute-start.6 = (f32[3,1,16,32]{3,2,1,0:T(8,128)}, f32[3,1,16,32]{3,2,1,0:T(8,128)}, u32[]{:S(2)}, u32[]{:S(2)}) collective-permute-start(f32[3,1,16,32]{3,2,1,0:T(8,128)} %get-tuple-element.185), channel_id=1, source_target_pairs={{0,1},{1,2},{2,3},{3,4},{4,5},{5,6},{6,7},{8,9},{9,10},{10,11},{11... | collective-permute-start | bytes 18440 | tf_op jit(solution)/shard_map/ppermute | solution.py:23
  53.7 1.4 fusion.51
  55.2 1.4 fusion.50
  56.6 1.4 fusion.49
  58.0 1.4 fusion.52
  62.0 8.8 %all-gather = f32[12,2,16,32]{3,2,1,0:T(8,128)S(1)} all-gather(f32[3,2,16,32]{3,2,1,0:T(8,128)S(1)} %broadcast_multiply_fusion.1), channel_id=2, replica_groups=mesh['tm'=4,'space'=8] {'tm'}, dimensions={0}, use_global_device_ids=true | all-gather | bytes 61440 | tf_op jit(solution)/shard_map/all_gather | solution.py:113
  70.8 2.3 add_bitcast_fusion.3
  73.9 1.5 convolution_bitcast_fusion.3
  75.5 14.0 %psum.16 = f32[4,4]{0,1:T(4,128)S(1)} all-reduce(f32[4,4]{0,1:T(4,128)} %convolution_bitcast_fusion.3), channel_id=1, replica_groups=mesh['tm'=4,'space'=8] {'space'}, use_global_device_ids=true, to_apply=%region_2.3 | all-reduce | flops 16 | bytes 128 | tf_op jit(solution)/shard_map/psum | solution.py:119
  92.4 4.9 %fusion.21 = f32[3,8,64,128]{3,2,1,0:T(8,128)S(1)} fusion(f32[3,2,64,128]{3,2,1,0:T(8,128)} %collective-permute-done.4, f32[3,8,64,128]{3,2,1,0:T(8,128)S(1)} %bitcast.95, f32[3,2,64,128]{3,2,1,0:T(8,128)} %copy-done.7, f32[1,8,64,128]{3,2,1,0:T(8,128)} %get-tuple-element.155, f32[1,8,64,128]{3,2,1,0:T(8,128)} %get-tuple-element.154, ...), kind=kLoop, calls=%fused_computation.35 | loop fusion | flops 8060928 | bytes 9043968 | tf_op jit(solution)/shard_map/add | solution.py:104
  97.5 27.4 %reshape.319 = f32[3,2,4,16,4,32,4]{6,5,4,3,2,1,0:T(8,128)} reshape(f32[3,8,64,128]{3,2,1,0:T(8,128)S(1)} %fusion.21) | data formatting | bytes 1572864 | tf_op jit(solution)/shard_map/reshape | solution.py:65
  124.8 9.6 %reduce_sum.19 = f32[3,2,16,32]{3,2,1,0:T(8,128)S(1)} reduce(f32[3,2,4,16,4,32,4]{6,5,4,3,2,1,0:T(8,128)} %reshape.319, f32[]{:T(128)} %constant.87.clone.1), dimensions={2,4,6}, to_apply=%region_0.1 | reduce | flops 193536 | bytes 798724 | tf_op jit(solution)/shard_map/reduce_sum | solution.py:68
  135.4 8.6 %all-gather.1 = f32[12,2,16,32]{3,2,1,0:T(8,128)S(1)} all-gather(f32[3,2,16,32]{3,2,1,0:T(8,128)S(1)} %get-tuple-element.174), channel_id=3, replica_groups=mesh['tm'=4,'space'=8] {'tm'}, dimensions={0}, use_global_device_ids=true | all-gather | bytes 61440 | tf_op jit(solution)/shard_map/all_gather | solution.py:114
  144.1 75.7 %while.13 = (s32[]{:T(128)}, f32[3,2,16,32]{3,2,1,0:T(8,128)S(1)}, f32[4,4]{1,0:T(4,128)S(1)}, pred[]{:T(512)}, f32[3,2,16,32]{3,2,1,0:T(8,128)S(1)}, /*index=5*...) while((s32[]{:T(128)}, f32[3,2,16,32]{3,2,1,0:T(8,128)S(1)}, ...), condition=%wide.region_7.8_spmd.clone, body=%wide.region_5.7_spmd.clone.sunk | while | flops 356775 | bytes 639592 | solution.py:134
  144.1 2.7 %collective-permute-start = (f32[3,2,16,32]{3,2,1,0:T(8,128)S(1)}, f32[3,2,16,32]{3,2,1,0:T(8,128)S(1)}, u32[]{:S(2)}, u32[]{:S(2)}) collective-permute-start(f32[3,2,16,32]{3,2,1,0:T(8,128)S(1)} %select_add_fusion.2), channel_id=1, source_target_pairs={{0,8},{8,16},{16,24},{1,9},{9,17},{17,25},{2,10},{10,18},{18,26},{... | collective-permute-start | bytes 36872 | tf_op jit(solution)/shard_map/while/body/eval_jaxpr/ppermute | solution.py:35
  149.2 13.6 %psum.19 = f32[4]{0:T(128)S(1)} all-reduce(f32[4]{0:T(128)S(1)} %convolution_bitcast_fusion.7), channel_id=1, replica_groups=mesh['tm'=4,'space'=8] {'space'}, use_global_device_ids=true, to_apply=%region_6.6 | all-reduce | flops 4 | bytes 32 | tf_op jit(solution)/shard_map/while/body/eval_jaxpr/psum | solution.py:125
  163.1 1.8 collective-permute-start.1
  164.9 1.3 collective-permute-start.2
  168.1 4.2 %collective-permute-start = (f32[3,2,16,32]{3,2,1,0:T(8,128)S(1)}, f32[3,2,16,32]{3,2,1,0:T(8,128)S(1)}, u32[]{:S(2)}, u32[]{:S(2)}) collective-permute-start(f32[3,2,16,32]{3,2,1,0:T(8,128)S(1)} %select_add_fusion.2), channel_id=1, source_target_pairs={{0,8},{8,16},{16,24},{1,9},{9,17},{17,25},{2,10},{10,18},{18,26},{... | collective-permute-start | bytes 36872 | tf_op jit(solution)/shard_map/while/body/eval_jaxpr/ppermute | solution.py:35
  174.7 14.9 %psum.19 = f32[4]{0:T(128)S(1)} all-reduce(f32[4]{0:T(128)S(1)} %convolution_bitcast_fusion.7), channel_id=1, replica_groups=mesh['tm'=4,'space'=8] {'space'}, use_global_device_ids=true, to_apply=%region_6.6 | all-reduce | flops 4 | bytes 32 | tf_op jit(solution)/shard_map/while/body/eval_jaxpr/psum | solution.py:125
  189.8 1.3 collective-permute-start.1
  191.1 1.3 collective-permute-start.2
  194.3 4.3 %collective-permute-start = (f32[3,2,16,32]{3,2,1,0:T(8,128)S(1)}, f32[3,2,16,32]{3,2,1,0:T(8,128)S(1)}, u32[]{:S(2)}, u32[]{:S(2)}) collective-permute-start(f32[3,2,16,32]{3,2,1,0:T(8,128)S(1)} %select_add_fusion.2), channel_id=1, source_target_pairs={{0,8},{8,16},{16,24},{1,9},{9,17},{17,25},{2,10},{10,18},{18,26},{... | collective-permute-start | bytes 36872 | tf_op jit(solution)/shard_map/while/body/eval_jaxpr/ppermute | solution.py:35
  200.9 14.1 %psum.19 = f32[4]{0:T(128)S(1)} all-reduce(f32[4]{0:T(128)S(1)} %convolution_bitcast_fusion.7), channel_id=1, replica_groups=mesh['tm'=4,'space'=8] {'space'}, use_global_device_ids=true, to_apply=%region_6.6 | all-reduce | flops 4 | bytes 32 | tf_op jit(solution)/shard_map/while/body/eval_jaxpr/psum | solution.py:125
  215.3 1.3 collective-permute-start.1
  216.6 1.3 collective-permute-start.2
  219.8 11.6 %broadcast_in_dim.8 = f32[3,2,4,16,4,32,4]{6,5,4,3,2,1,0:T(8,128)} broadcast(f32[3,2,16,32]{3,2,1,0:T(8,128)S(1)} %get-tuple-element.99), dimensions={0,1,3,5} | broadcast | bytes 798720 | tf_op jit(solution)/shard_map/broadcast_in_dim | solution.py:73
  231.4 21.4 %reshape.322 = f32[3,8,64,128]{3,2,1,0:T(8,128)S(1)} reshape(f32[3,2,4,16,4,32,4]{6,5,4,3,2,1,0:T(8,128)} %broadcast_in_dim.8) | data formatting | bytes 1572864 | tf_op jit(solution)/shard_map/reshape | solution.py:77
  (108 shorter events, 27.2 us)
Async XLA Ops:
  1.1 90.7 %collective-permute-start.3 = (f32[3,2,64,128]{3,2,1,0:T(8,128)S(1)}, f32[3,2,64,128]{3,2,1,0:T(8,128)S(1)}, u32[]{:S(2)}, u32[]{:S(2)}) collective-permute-start(f32[3,2,64,128]{3,2,1,0:T(8,128)S(1)} %get-tuple-element.172), channel_id=1, source_target_pairs={{1,0},{2,1},{3,2},{4,3},{5,4},{6,5},{7,6},{9,8},{10,9},{11,10},{12... | collective-permute-start | bytes 589832 | tf_op jit(solution)/shard_map/ppermute | solution.py:25
  2.4 48.7 %copy-start = (f32[1,3,8,64,128]{4,3,2,1,0:T(8,128)S(1)}, f32[1,3,8,64,128]{4,3,2,1,0:T(8,128)}, u32[]{:S(2)}) copy-start(f32[1,3,8,64,128]{4,3,2,1,0:T(8,128)} %param.4) | copy-start | bytes 2359300
  2.4 89.4 %collective-permute-start.4 = (f32[3,2,64,128]{3,2,1,0:T(8,128)S(1)}, f32[3,2,64,128]{3,2,1,0:T(8,128)}, u32[]{:S(2)}, u32[]{:S(2)}) collective-permute-start(f32[3,2,64,128]{3,2,1,0:T(8,128)S(1)} %get-tuple-element.173), channel_id=1, source_target_pairs={{0,1},{1,2},{2,3},{3,4},{4,5},{5,6},{6,7},{8,9},{9,10},{10,11},{11... | collective-permute-start | bytes 589832 | tf_op jit(solution)/shard_map/ppermute | solution.py:23
  44.6 89.8 %collective-permute-start.5 = (f32[3,1,16,32]{3,2,1,0:T(8,128)}, f32[3,1,16,32]{3,2,1,0:T(8,128)}, u32[]{:S(2)}, u32[]{:S(2)}) collective-permute-start(f32[3,1,16,32]{3,2,1,0:T(8,128)} %get-tuple-element.184), channel_id=1, source_target_pairs={{1,0},{2,1},{3,2},{4,3},{5,4},{6,5},{7,6},{9,8},{10,9},{11,10},{12... | collective-permute-start | bytes 18440 | tf_op jit(solution)/shard_map/ppermute | solution.py:25
  45.9 88.5 %collective-permute-start.6 = (f32[3,1,16,32]{3,2,1,0:T(8,128)}, f32[3,1,16,32]{3,2,1,0:T(8,128)}, u32[]{:S(2)}, u32[]{:S(2)}) collective-permute-start(f32[3,1,16,32]{3,2,1,0:T(8,128)} %get-tuple-element.185), channel_id=1, source_target_pairs={{0,1},{1,2},{2,3},{3,4},{4,5},{5,6},{6,7},{8,9},{9,10},{10,11},{11... | collective-permute-start | bytes 18440 | tf_op jit(solution)/shard_map/ppermute | solution.py:23
  91.7 0.7 copy-start.7
  97.4 37.0 %copy-start.1 = (f32[3,2,15,32]{3,2,1,0:T(8,128)S(1)}, f32[3,2,15,32]{3,2,1,0:T(8,128)}, u32[]{:S(2)}) copy-start(f32[3,2,15,32]{3,2,1,0:T(8,128)} %get-tuple-element.180) | copy-start | bytes 34564
  97.4 37.0 %copy-start.2 = (f32[3,2,15,32]{3,2,1,0:T(8,128)S(1)}, f32[3,2,15,32]{3,2,1,0:T(8,128)}, u32[]{:S(2)}) copy-start(f32[3,2,15,32]{3,2,1,0:T(8,128)} %get-tuple-element.181) | copy-start | bytes 34564
  97.4 37.0 %copy-start.3 = (f32[3,2,16,1]{3,2,1,0:T(8,128)S(1)}, f32[3,2,16,1]{3,2,1,0:T(8,128)}, u32[]{:S(2)}) copy-start(f32[3,2,16,1]{3,2,1,0:T(8,128)} %get-tuple-element.178) | copy-start | bytes 1156
  97.4 37.0 %copy-start.4 = (f32[3,2,16,1]{3,2,1,0:T(8,128)S(1)}, f32[3,2,16,1]{3,2,1,0:T(8,128)}, u32[]{:S(2)}) copy-start(f32[3,2,16,1]{3,2,1,0:T(8,128)} %get-tuple-element.179) | copy-start | bytes 1156
  97.4 37.0 %copy-start.5 = (f32[3,2,16,31]{3,2,1,0:T(8,128)S(1)}, f32[3,2,16,31]{3,2,1,0:T(8,128)}, u32[]{:S(2)}) copy-start(f32[3,2,16,31]{3,2,1,0:T(8,128)} %get-tuple-element.176) | copy-start | bytes 35716
  97.4 37.0 %copy-start.6 = (f32[3,2,16,31]{3,2,1,0:T(8,128)S(1)}, f32[3,2,16,31]{3,2,1,0:T(8,128)}, u32[]{:S(2)}) copy-start(f32[3,2,16,31]{3,2,1,0:T(8,128)} %get-tuple-element.177) | copy-start | bytes 35716
  97.4 37.0 %copy-start.10 = (f32[3,2,1,32]{3,2,1,0:T(1,128)S(1)}, f32[3,2,1,32]{3,2,1,0:T(1,128)}, u32[]{:S(2)}) copy-start(f32[3,2,1,32]{3,2,1,0:T(1,128)} %get-tuple-element.182) | copy-start | bytes 2308
  97.4 37.0 %copy-start.11 = (f32[3,2,1,32]{3,2,1,0:T(1,128)S(1)}, f32[3,2,1,32]{3,2,1,0:T(1,128)}, u32[]{:S(2)}) copy-start(f32[3,2,1,32]{3,2,1,0:T(1,128)} %get-tuple-element.183) | copy-start | bytes 2308
  97.4 46.6 %copy-start.8 = (f32[4,4]{1,0:T(4,128)S(1)}, f32[4,4]{1,0:T(4,128)}, u32[]{:S(2)}) copy-start(f32[4,4]{1,0:T(4,128)} %select_select_fusion) | copy-start | bytes 196
  97.5 46.6 %copy-start.9 = (f32[4,3072]{1,0:T(4,128)S(1)}, f32[4,3072]{1,0:T(4,128)}, u32[]{:S(2)}) copy-start(f32[4,3072]{1,0:T(4,128)} %reshape.320) | copy-start | bytes 147460
  144.1 4.5 %collective-permute-start = (f32[3,2,16,32]{3,2,1,0:T(8,128)S(1)}, f32[3,2,16,32]{3,2,1,0:T(8,128)S(1)}, u32[]{:S(2)}, u32[]{:S(2)}) collective-permute-start(f32[3,2,16,32]{3,2,1,0:T(8,128)S(1)} %select_add_fusion.2), channel_id=1, source_target_pairs={{0,8},{8,16},{16,24},{1,9},{9,17},{17,25},{2,10},{10,18},{18,26},{... | collective-permute-start | bytes 36872 | tf_op jit(solution)/shard_map/while/body/eval_jaxpr/ppermute | solution.py:35
  163.1 3.7 %collective-permute-start.1 = (f32[3,1,16,32]{3,2,1,0:T(8,128)S(1)}, f32[3,1,16,32]{3,2,1,0:T(8,128)S(1)}, u32[]{:S(2)}, u32[]{:S(2)}) collective-permute-start(f32[3,1,16,32]{3,2,1,0:T(8,128)S(1)} %get-tuple-element.245), channel_id=1, source_target_pairs={{0,1},{1,2},{2,3},{3,4},{4,5},{5,6},{6,7},{8,9},{9,10},{10,11},{11... | collective-permute-start | bytes 18440 | tf_op jit(solution)/shard_map/while/body/eval_jaxpr/ppermute | solution.py:23
  164.9 3.1 %collective-permute-start.2 = (f32[3,1,16,32]{3,2,1,0:T(8,128)S(1)}, f32[3,1,16,32]{3,2,1,0:T(8,128)S(1)}, u32[]{:S(2)}, u32[]{:S(2)}) collective-permute-start(f32[3,1,16,32]{3,2,1,0:T(8,128)S(1)} %get-tuple-element.246), channel_id=1, source_target_pairs={{1,0},{2,1},{3,2},{4,3},{5,4},{6,5},{7,6},{9,8},{10,9},{11,10},{12... | collective-permute-start | bytes 18440 | tf_op jit(solution)/shard_map/while/body/eval_jaxpr/ppermute | solution.py:25
  168.1 6.0 %collective-permute-start = (f32[3,2,16,32]{3,2,1,0:T(8,128)S(1)}, f32[3,2,16,32]{3,2,1,0:T(8,128)S(1)}, u32[]{:S(2)}, u32[]{:S(2)}) collective-permute-start(f32[3,2,16,32]{3,2,1,0:T(8,128)S(1)} %select_add_fusion.2), channel_id=1, source_target_pairs={{0,8},{8,16},{16,24},{1,9},{9,17},{17,25},{2,10},{10,18},{18,26},{... | collective-permute-start | bytes 36872 | tf_op jit(solution)/shard_map/while/body/eval_jaxpr/ppermute | solution.py:35
  189.8 3.2 %collective-permute-start.1 = (f32[3,1,16,32]{3,2,1,0:T(8,128)S(1)}, f32[3,1,16,32]{3,2,1,0:T(8,128)S(1)}, u32[]{:S(2)}, u32[]{:S(2)}) collective-permute-start(f32[3,1,16,32]{3,2,1,0:T(8,128)S(1)} %get-tuple-element.245), channel_id=1, source_target_pairs={{0,1},{1,2},{2,3},{3,4},{4,5},{5,6},{6,7},{8,9},{9,10},{10,11},{11... | collective-permute-start | bytes 18440 | tf_op jit(solution)/shard_map/while/body/eval_jaxpr/ppermute | solution.py:23
  191.1 3.1 %collective-permute-start.2 = (f32[3,1,16,32]{3,2,1,0:T(8,128)S(1)}, f32[3,1,16,32]{3,2,1,0:T(8,128)S(1)}, u32[]{:S(2)}, u32[]{:S(2)}) collective-permute-start(f32[3,1,16,32]{3,2,1,0:T(8,128)S(1)} %get-tuple-element.246), channel_id=1, source_target_pairs={{1,0},{2,1},{3,2},{4,3},{5,4},{6,5},{7,6},{9,8},{10,9},{11,10},{12... | collective-permute-start | bytes 18440 | tf_op jit(solution)/shard_map/while/body/eval_jaxpr/ppermute | solution.py:25
  194.3 6.0 %collective-permute-start = (f32[3,2,16,32]{3,2,1,0:T(8,128)S(1)}, f32[3,2,16,32]{3,2,1,0:T(8,128)S(1)}, u32[]{:S(2)}, u32[]{:S(2)}) collective-permute-start(f32[3,2,16,32]{3,2,1,0:T(8,128)S(1)} %select_add_fusion.2), channel_id=1, source_target_pairs={{0,8},{8,16},{16,24},{1,9},{9,17},{17,25},{2,10},{10,18},{18,26},{... | collective-permute-start | bytes 36872 | tf_op jit(solution)/shard_map/while/body/eval_jaxpr/ppermute | solution.py:35
  215.3 3.2 %collective-permute-start.1 = (f32[3,1,16,32]{3,2,1,0:T(8,128)S(1)}, f32[3,1,16,32]{3,2,1,0:T(8,128)S(1)}, u32[]{:S(2)}, u32[]{:S(2)}) collective-permute-start(f32[3,1,16,32]{3,2,1,0:T(8,128)S(1)} %get-tuple-element.245), channel_id=1, source_target_pairs={{0,1},{1,2},{2,3},{3,4},{4,5},{5,6},{6,7},{8,9},{9,10},{10,11},{11... | collective-permute-start | bytes 18440 | tf_op jit(solution)/shard_map/while/body/eval_jaxpr/ppermute | solution.py:23
  216.6 3.1 %collective-permute-start.2 = (f32[3,1,16,32]{3,2,1,0:T(8,128)S(1)}, f32[3,1,16,32]{3,2,1,0:T(8,128)S(1)}, u32[]{:S(2)}, u32[]{:S(2)}) collective-permute-start(f32[3,1,16,32]{3,2,1,0:T(8,128)S(1)} %get-tuple-element.246), channel_id=1, source_target_pairs={{1,0},{2,1},{3,2},{4,3},{5,4},{6,5},{7,6},{9,8},{10,9},{11,10},{12... | collective-permute-start | bytes 18440 | tf_op jit(solution)/shard_map/while/body/eval_jaxpr/ppermute | solution.py:25
where the time goes:
time: 259 us; the launch traced here: 254 us
  local copies, waits for them, and re-layouts  104 us (40%)
  blocking collectives  74 us (29%)
  other arithmetic  31.8 us (12%)
  starting transfers between devices  31.1 us (12%)
  waiting for transfers between devices  7.44 us (3%)
  matrix products  4.78 us (2%)
    psum x3, blocking collectives, kapply(): coeffs = solve_small(factor, lax.psum(product, 'space'))  42.6 us
    another operation x1, local copies, waits for them, and re-layouts, restrict_field(): field.reshape(comps, depth // COARSEN, COARSEN, width_x // COARSEN, COARS...  28.2 us
    reshape x1, local copies, waits for them, and re-layouts, restrict_field(): field.reshape(comps, depth // COARSEN, COARSEN, width_x // COARSEN, COARS...  27.4 us
    reshape x1, local copies, waits for them, and re-layouts, prolong_field(): spread.reshape(comps, depth * COARSEN, width_x * COARSEN, width_y * COARSEN)  21.4 us
    reduce_sum x2, other arithmetic, restrict_field(): return jnp.mean(blocks, axis=(2, 4, 6))  19.1 us
    psum x1, blocking collectives, local(): gram_matrix = lax.psum(local_gram, 'space')  14 us
    ppermute x5, starting transfers between devices, padded_2(): lax.ppermute(tail, axis, [(i, (i + 1) % count) for i in range(ends)])  13.4 us
    broadcast_in_dim x1, local copies, waits for them, and re-layouts, prolong_field(): jnp.broadcast_to(coarse[:, :, None, :, None, :, None], (comps, depth, COA...  11.6 us
  transfers between devices with their start and end apart: 13, of which 6 were waited for; matrix products, arithmetic and copies ran while one was open for 40% of the time, Pallas kernels for 0%

commit v1 on v0

v1 whole, which is shorter than its diff:
```python
import functools

import jax
import jax.numpy as jnp
from jax import lax
from jax.experimental import pallas as pl
from jax.experimental.pallas import tpu as pltpu
from jax.sharding import PartitionSpec as P

COARSEN = 4
NEAR = 0.8
FAR = 0.2
DIFFUSION = 0.08
RATE = 0.1
LANES = 128
HI = lax.Precision.HIGHEST
MESH = pl.DeviceIdType.MESH


def iota(shape, dim):
    return lax.broadcasted_iota(jnp.int32, shape, dim)


def dot(a, b, dims=((1,), (0,))):
    return lax.dot_general(a, b, (dims, ((), ())), precision=HI, preferred_element_type=jnp.float32)


def pick(condition):
    return jnp.where(condition, 1.0, 0.0).astype(jnp.float32)


class Plan:
    def __init__(self, slices, slabs, block):
        self.S, self.Z = slices, slabs
        self.C, self.D, self.X, self.Y = block
        self.p = self.D // COARSEN
        self.nx, self.ny = self.X // COARSEN, self.Y // COARSEN
        self.groups = LANES // self.ny
        self.rp = self.nx // self.groups
        self.rows = self.p * self.rp
        self.H = min(slabs - 1, -(-(slices - 1) // self.p))
        self.W = 2 * self.H + 1
        self.N = slices * slabs
        self.count = 2 * (slices - 1) * slices
        self.LQ = -(-self.count // LANES) * LANES


def step_tools(plan):
    shape = (plan.rows, LANES)
    row, lane = iota(shape, 0), iota(shape, 1)
    low = row % plan.rp
    y = lane % plan.ny
    return dict(
        last_y=y == plan.ny - 1,
        first_y=y == 0,
        last_x=low == plan.rp - 1,
        first_x=low == 0,
        last_z=row >= plan.rows - plan.rp,
        first_z=row < plan.rp,
    )


def coarse_step(plan, tools, prev, cur, nxt):
    rows, rp, ny = plan.rows, plan.rp, plan.ny
    roll = pltpu.roll
    total = jnp.where(tools["last_y"], roll(cur, ny - 1, 1), roll(cur, LANES - 1, 1))
    total += jnp.where(tools["first_y"], roll(cur, LANES - ny + 1, 1), roll(cur, 1, 1))
    total += jnp.where(
        tools["last_x"], roll(roll(cur, rp - 1, 0), LANES - ny, 1), roll(cur, rows - 1, 0)
    )
    total += jnp.where(
        tools["first_x"], roll(roll(cur, rows - rp + 1, 0), ny, 1), roll(cur, 1, 0)
    )
    up = roll(cur, rows - rp, 0)
    down = roll(cur, rp, 0)
    zero = jnp.zeros_like(cur)
    above = zero if nxt is None else roll(nxt, rows - rp, 0)
    below = zero if prev is None else roll(prev, rp, 0)
    total += jnp.where(tools["last_z"], above, up) + jnp.where(tools["first_z"], below, down)
    return cur + RATE * (total - 6.0 * cur)


def kernel(
    plan, start_hbm, strain_hbm, fine_hbm, add_ref,
    f, st, o, bx, ix, prod, mbuf,
    in_sem, out_sem, halo_send, halo_recv, b_send, b_recv, i_send, i_recv, m_send, m_recv,
):
    S, Z, C, D, X, Y, H, W, N = (
        plan.S, plan.Z, plan.C, plan.D, plan.X, plan.Y, plan.H, plan.W, plan.N
    )
    p, rows, groups, rp, ny = plan.p, plan.rows, plan.groups, plan.rp, plan.ny
    t, s = lax.axis_index("tm"), lax.axis_index("space")
    me = s * S + t

    load_start = pltpu.make_async_copy(start_hbm.at[0], f.at[:, pl.ds(2, D)], in_sem.at[0])
    load_start.start()
    load_strain = pltpu.make_async_copy(strain_hbm.at[0], st, in_sem.at[1])
    load_strain.start()

    barrier = pltpu.get_barrier_semaphore()

    def greet(k, carry):
        peer = lax.rem(me + k, N)
        pl.semaphore_signal(
            barrier, inc=1, device_id=(lax.rem(peer, S), peer // S), device_id_type=MESH
        )
        return carry

    lax.fori_loop(1, N, greet, 0)

    spread_y = pick(iota((Y, LANES), 0) // COARSEN == iota((Y, LANES), 1) % ny)
    tall = (groups * rows, p * X)
    a, b = iota(tall, 0), iota(tall, 1)
    coarse_x = (a // rows) * rp + a % rp
    gather_x = pick(((a % rows) // rp == b // X) & ((b % X) // COARSEN == coarse_x))
    group_of = iota((rows, LANES), 1) // ny

    def restrict(plane_sums):
        wide = dot(jnp.concatenate(plane_sums, axis=0), spread_y)
        result = []
        for c in range(C):
            tallc = dot(gather_x, wide[c * p * X : (c + 1) * p * X])
            total = jnp.zeros((rows, LANES), jnp.float32)
            for g in range(groups):
                total += jnp.where(group_of == g, tallc[g * rows : (g + 1) * rows], 0.0)
            result.append(total * (1.0 / COARSEN**3))
        return result

    load_start.wait()
    sums = []
    for c in range(C):
        planes = []
        for zz in range(p):
            base = 2 + zz * COARSEN
            acc = f[c, base]
            for k in range(1, COARSEN):
                acc = acc + f[c, base + k]
            planes.append(acc)
        sums.append(jnp.concatenate(planes, axis=0))
    own_b = restrict(sums)
    for c in range(C):
        bx[H, t, c] = own_b[c]

    for d in range(-H, H + 1):
        if d != 0:

            @pl.when((s + d < 0) | (s + d >= Z))
            def _():
                bx[H + d] = jnp.zeros((S, C, rows, LANES), jnp.float32)
                ix[H + d] = jnp.zeros((S, C, rows, LANES), jnp.float32)

    @pl.when(s == 0)
    def _():
        f[:, 0:2] = jnp.zeros((C, 2, X, Y), jnp.float32)

    @pl.when(s == Z - 1)
    def _():
        f[:, D + 2 : D + 4] = jnp.zeros((C, 2, X, Y), jnp.float32)

    pl.semaphore_wait(barrier, N - 1)

    up_copy = pltpu.make_async_remote_copy(
        src_ref=f.at[:, pl.ds(D, 2)], dst_ref=f.at[:, pl.ds(0, 2)],
        send_sem=halo_send.at[0], recv_sem=halo_recv.at[0],
        device_id=(t, jnp.minimum(s + 1, Z - 1)), device_id_type=MESH,
    )
    down_copy = pltpu.make_async_remote_copy(
        src_ref=f.at[:, pl.ds(2, 2)], dst_ref=f.at[:, pl.ds(D + 2, 2)],
        send_sem=halo_send.at[1], recv_sem=halo_recv.at[1],
        device_id=(t, jnp.maximum(s - 1, 0)), device_id_type=MESH,
    )

    def share(buf, send, recv):
        order = sorted(range(-H, H + 1), key=abs)
        for d in order:

            def one(k, carry):
                pltpu.make_async_remote_copy(
                    src_ref=buf.at[H, t], dst_ref=buf.at[H - d, t],
                    send_sem=send.at[H + d], recv_sem=recv.at[H - d],
                    device_id=(lax.rem(t + k, S), s + d), device_id_type=MESH,
                ).start()
                return carry

            @pl.when((s + d >= 0) & (s + d < Z))
            def _():
                lax.fori_loop(1 if d == 0 else 0, S, one, 0)

    def settle(buf, sem):
        for d in range(-H, H + 1):
            size = S - 1 if d == 0 else S

            @pl.when((s + d >= 0) & (s + d < Z))
            def _():
                view = buf.at[H + d, pl.ds(0, size)]
                pltpu.make_async_copy(view, view, sem.at[H + d]).wait()

    share(bx, b_send, b_recv)

    @pl.when(s < Z - 1)
    def _():
        up_copy.start()

    @pl.when(s > 0)
    def _():
        down_copy.start()

    load_strain.wait()

    @pl.when(s > 0)
    def _():
        up_copy.wait_recv()

    @pl.when(s < Z - 1)
    def _():
        down_copy.wait_recv()

    near, far = DIFFUSION * NEAR, DIFFUSION * FAR
    centre = 1.0 - 6.0 * (near + far)

    def fine_plane(z, carry):
        v = [f[c, z + 2] for c in range(C)]
        for c in range(C):
            n1 = f[c, z + 1] + f[c, z + 3]
            n2 = f[c, z] + f[c, z + 4]
            n1 += pltpu.roll(v[c], 1, 0) + pltpu.roll(v[c], X - 1, 0)
            n2 += pltpu.roll(v[c], 2, 0) + pltpu.roll(v[c], X - 2, 0)
            n1 += pltpu.roll(v[c], 1, 1) + pltpu.roll(v[c], Y - 1, 1)
            n2 += pltpu.roll(v[c], 2, 1) + pltpu.roll(v[c], Y - 2, 1)
            acc = centre * v[c] + near * n1 + far * n2
            for j in range(C):
                acc += st[C * c + j, z].astype(jnp.float32) * v[j]
            o[c, z] = acc
        return carry

    lax.fori_loop(0, D, fine_plane, 0)
    store_fine = pltpu.make_async_copy(o, fine_hbm, out_sem)
    store_fine.start()

    sums = []
    for c in range(C):
        planes = []
        for zz in range(p):
            acc = o[c, zz * COARSEN]
            for k in range(1, COARSEN):
                acc = acc + o[c, zz * COARSEN + k]
            planes.append(acc)
        sums.append(jnp.concatenate(planes, axis=0))
    own_i = restrict(sums)
    for c in range(C):
        ix[H, t, c] = own_i[c]
    share(ix, i_send, i_recv)

    settle(bx, b_recv)
    tools = step_tools(plan)
    inside = [(s + d >= 0) & (s + d < Z) for d in range(-H, H + 1)]

    def advance(m_fields, reach):
        result = {}
        for d in range(-reach, reach + 1):
            out = coarse_step(plan, tools, m_fields.get(d - 1), m_fields[d], m_fields.get(d + 1))
            result[d] = out if d == 0 else jnp.where(inside[H + d], out, 0.0)
        return result

    prod[...] = jnp.zeros(prod.shape, jnp.float32)

    def powers(m, carry):
        sums_i = [None] * (S - 1)
        sums_b = [None] * (S - 1)
        for c in range(C):
            reach = min(H, -(-(S - 2) // p))
            fields = {d: bx[H + d, m, c] for d in range(-reach, reach + 1)}
            for k in range(S - 1):
                if k > 0:
                    fields = advance(fields, min(H, -(-(S - 2 - k) // p)))
                ti, tb = fields[0] * own_i[c], fields[0] * own_b[c]
                sums_i[k] = ti if c == 0 else sums_i[k] + ti
                sums_b[k] = tb if c == 0 else sums_b[k] + tb
        for k in range(S - 1):
            prod[k * S + m] = jnp.sum(sums_i[k], axis=0, keepdims=True)
            prod[(S - 1 + k) * S + m] = jnp.sum(sums_b[k], axis=0, keepdims=True)
        return carry

    if S <= 4:
        for m in range(S):
            powers(m, 0)
    else:
        lax.fori_loop(0, S, powers, 0)
    message = dot(jnp.ones((8, LANES), jnp.float32), prod[:, 0, :], ((1,), (1,)))
    mbuf[me] = message[0:1]

    def tell(k, carry):
        peer = lax.rem(me + k, N)
        pltpu.make_async_remote_copy(
            src_ref=mbuf.at[me], dst_ref=mbuf.at[me], send_sem=m_send, recv_sem=m_recv,
            device_id=(lax.rem(peer, S), peer // S), device_id_type=MESH,
        ).start()
        return carry

    lax.fori_loop(1, N, tell, 0)
    view = mbuf.at[pl.ds(0, N - 1)]
    pltpu.make_async_copy(view, view, m_recv).wait()
    owner = pick(iota((N, LANES), 0) % S == iota((N, LANES), 1))
    table = dot(mbuf[:, 0, :], owner, ((0,), (0,)))

    def block(kind, k):
        at = (kind * (S - 1) + k) * S
        return table[at : at + S]

    row, lane = iota((S, LANES), 0), iota((S, LANES), 1)
    lane1 = iota((1, LANES), 1)
    swept = block(1, 0)
    for i in range(S):
        pivot_row = swept[i : i + 1]
        pivot_col = jnp.sum(jnp.where(lane == i, swept, 0.0), axis=1, keepdims=True)
        pivot = jnp.sum(jnp.where(lane1 == i, pivot_row, 0.0), axis=1, keepdims=True)
        inv = 1.0 / pivot
        body = swept - pivot_col * (pivot_row * inv)
        body = jnp.where(row == i, pivot_row * inv, body)
        body = jnp.where(lane == i, pivot_col * inv, body)
        swept = jnp.where((row == i) & (lane == i), -inv, body)
    inverse = -swept
    mats = [block(0, k) - block(1, k + 1) for k in range(S - 2)]
    coeffs = []
    for j in range(1, S):
        p_col = jnp.sum(jnp.where(lane == 0, block(0, j - 1), 0.0), axis=1, keepdims=True)
        if j > 1:
            terms = jnp.zeros((S, LANES), jnp.float32)
            for i in range(1, j):
                terms += mats[j - 1 - i] * coeffs[i - 1]
            p_col = p_col + jnp.sum(terms, axis=1, keepdims=True)
        coeffs.append(
            jnp.where(lane1 < S, jnp.sum(inverse * p_col, axis=0, keepdims=True), 0.0)
        )

    settle(ix, i_recv)

    carried = []
    weights = [
        [jnp.sum(jnp.where(lane1 == m, coeffs[j], 0.0), axis=1, keepdims=True) for m in range(S)]
        for j in range(S - 1)
    ]
    for c in range(C):
        w = {d: ix[H + d, 0, c] for d in range(-H, H + 1)}
        mine = w[0]
        for j in range(1, S):
            reach = min(H, -(-(S - 1 - j) // p))
            source = min(H, reach + 1)
            left = {}
            for d in range(-source, source + 1):
                if d not in w:
                    continue
                value = w[d]
                for m in range(S):
                    value = value - weights[j - 1][m] * bx[H + d, m, c]
                left[d] = value
            moved = advance(left, reach)
            w = {}
            for d in range(-reach, reach + 1):
                value = moved[d]
                for m in range(S):
                    value = value + weights[j - 1][m] * ix[H + d, m, c]
                w[d] = value
            mine = jnp.where(t == j, w[0], mine)
        carried.append(mine - own_i[c])

    for c in range(C):
        stack = jnp.concatenate(
            [jnp.where(group_of == g, carried[c], 0.0) for g in range(groups)], axis=0
        )
        tallc = dot(gather_x, stack, ((0,), (0,)))
        full = dot(tallc, spread_y, ((1,), (1,)))
        for zz in range(p):
            add_ref[c, zz] = full[zz * X : (zz + 1) * X]

    store_fine.wait()
    settle(bx, b_send)
    settle(ix, i_send)
    pltpu.make_async_copy(view, view, m_send).wait()

    @pl.when(s < Z - 1)
    def _():
        up_copy.wait_send()

    @pl.when(s > 0)
    def _():
        down_copy.wait_send()


def local(starts, strain):
    slices, slabs = lax.axis_size("tm"), lax.axis_size("space")
    plan = Plan(slices, slabs, starts.shape[1:])
    C, D, X, Y = starts.shape[1:]
    f32 = jnp.float32
    coarse = (plan.W, plan.S, C, plan.rows, LANES)
    dma = pltpu.SemaphoreType.DMA
    fine, add = pl.pallas_call(
        functools.partial(kernel, plan),
        out_shape=(
            jax.ShapeDtypeStruct((C, D, X, Y), f32),
            jax.ShapeDtypeStruct((C, plan.p, X, Y), f32),
        ),
        in_specs=[pl.BlockSpec(memory_space=pl.ANY)] * 2,
        out_specs=(
            pl.BlockSpec(memory_space=pl.ANY),
            pl.BlockSpec(memory_space=pltpu.VMEM),
        ),
        scratch_shapes=[
            pltpu.VMEM((C, D + 4, X, Y), f32),
            pltpu.VMEM(strain.shape[1:], strain.dtype),
            pltpu.VMEM((C, D, X, Y), f32),
            pltpu.VMEM(coarse, f32),
            pltpu.VMEM(coarse, f32),
            pltpu.VMEM((plan.LQ, 1, LANES), f32),
            pltpu.VMEM((plan.N, 1, plan.LQ), f32),
            dma((2,)), dma(()), dma((2,)), dma((2,)),
            dma((plan.W,)), dma((plan.W,)), dma((plan.W,)), dma((plan.W,)),
            dma(()), dma(()),
        ],
        compiler_params=pltpu.CompilerParams(collective_id=0, has_side_effects=True),
    )(starts, strain)
    shape = (C, plan.p, COARSEN, X, Y)
    return (fine.reshape(shape) + add[:, :, None]).reshape(1, C, D, X, Y)


def solution(mesh):
    return jax.shard_map(
        local,
        mesh=mesh,
        in_specs=(P("tm", None, "space", None, None), P("tm", None, "space", None, None)),
        out_specs=P("tm", None, "space", None, None),
        check_vma=False,
    )
```

time: 259 us -> 24.6 us (0.09); the launches traced: 254 us -> 24.4 us
  local copies, waits for them, and re-layouts: 104 us -> 1.21 us
  blocking collectives: 74 us -> 0 us
  starting transfers between devices: 31.1 us -> 0 us
  other arithmetic: 31.8 us -> 1 us
  Pallas kernels: 0 us -> 22.2 us
  waiting for transfers between devices: 7.44 us -> 0 us
  matrix products: 4.78 us -> 0 us
    psum x4 -> x0, blocking collectives: 56.6 us -> none  [the longest x3 42.6 us: kapply(): coeffs = solve_small(factor, lax.psum(product, 'space'))]
    reshape x7 -> x0, local copies, waits for them, and re-layouts: 49.9 us -> none  [the longest x1 27.4 us: restrict_field(): field.reshape(comps, depth // COARSEN, COARSEN, width_x // COARSEN, COARS...]
    ppermute x13 -> x0, starting transfers between devices: 31.1 us -> none  [the longest x5 13.4 us: padded_2(): lax.ppermute(tail, axis, [(i, (i + 1) % count) for i in range(ends)])]
    another operation x1 -> x0, local copies, waits for them, and re-layouts: 28.2 us -> none  [restrict_field(): field.reshape(comps, depth // COARSEN, COARSEN, width_x // COARSEN, COARS...]
    pallas_call x0 -> x1, Pallas kernels: none -> 22.2 us  [local(): pl.pallas_call(functools.partial(kernel, plan), out_shape=(jax.ShapeDtype...]
    reduce_sum x2 -> x0, other arithmetic: 19.1 us -> none  [restrict_field(): return jnp.mean(blocks, axis=(2, 4, 6))]
    all_gather x2 -> x0, blocking collectives: 17.4 us -> none  [the longest x1 8.81 us: local(): lax.all_gather(start_coarse[None], 'tm', axis=0, tiled=True)]
    slice x29 -> x0, local copies, waits for them, and re-layouts: 13.2 us -> none  [the longest x4 4.71 us: plane_terms(): jnp.roll(field, -2, along)]
  transfers between devices with their start and end apart: 13 -> 0, of which waited for: 6 -> 0; matrix products, arithmetic and copies ran while one was open for 40% -> 0% of each run, Pallas kernels for 0% -> 0%
where the time goes in v1:
time: 24.6 us; the launch traced here: 24.4 us
  Pallas kernels  22.2 us (90%)
  local copies, waits for them, and re-layouts  1.21 us (5%)
  other arithmetic  1 us (4%)
    pallas_call x1, Pallas kernels, local(): pl.pallas_call(functools.partial(kernel, plan), out_shape=(jax.ShapeDtype...  22.2 us
    add x1, local copies, waits for them, and re-layouts, local(): return (fine.reshape(shape) + add[:, :, None]).reshape(1, C, D, X, Y)  1.07 us
    add x1, other arithmetic, local(): return (fine.reshape(shape) + add[:, :, None]).reshape(1, C, D, X, Y)  1 us

profile of v1, /device:TPU:0, one launch (start us, length us, event | category | flops | bytes accessed | tf_op | source)
XLA Modules:
  0.0 24.4 jit_solution(4354310195764408591)
XLA Ops:
  0.0 22.2 %shard_map.28 = (f32[3,8,64,128]{3,2,1,0:T(8,128)}, f32[3,2,64,128]{3,2,1,0:T(8,128)}) custom-call(f32[1,3,8,64,128]{4,3,2,1,0:T(8,128)} %start_hbm.1, bf16[1,9,8,64,128]{4,3,2,1,0:T(8,128)(2,1)} %strain_hbm.1), custom_call_target="tpu_custom_call" | custom-call | tf_op jit(solution)/shard_map/pallas_call | solution.py:397
  22.2 0.0 copy-start
  22.2 1.1 %add.14 = f32[3,2,4,64,128]{4,3,2,1,0:T(8,128)S(1)} broadcast(f32[3,2,64,128]{3,2,1,0:T(8,128)} %get-tuple-element.8), dimensions={0,1,3,4} | broadcast | bytes 983040 | tf_op jit(solution)/shard_map/add | solution.py:423
  23.3 0.1 copy-done
  23.4 1.0 %add_bitcast_fusion = f32[1,3,8,64,128]{4,3,2,1,0:T(8,128)} fusion(f32[3,8,64,128]{3,2,1,0:T(8,128)S(1)} %copy-done, f32[3,8,64,128]{3,2,1,0:T(8,128)S(1)} %bitcast.3), kind=kLoop, calls=%fused_computation | loop fusion | flops 196608 | bytes 2359296 | tf_op jit(solution)/shard_map/add | solution.py:423
Async XLA Ops:
  22.2 1.2 %copy-start = (f32[3,8,64,128]{3,2,1,0:T(8,128)S(1)}, f32[3,8,64,128]{3,2,1,0:T(8,128)}, u32[]{:S(2)}) copy-start(f32[3,8,64,128]{3,2,1,0:T(8,128)} %get-tuple-element.7) | copy-start | bytes 2359300

commit v2 on v1

--- a/solution.py
+++ b/solution.py
@@ -40,7 +40,8 @@
         self.rows = self.p * self.rp
         self.H = min(slabs - 1, -(-(slices - 1) // self.p))
         self.W = 2 * self.H + 1
-        self.N = slices * slabs
+        self.R = min(self.H, -(-(slices - 2) // self.p))
+        self.SP = -(-slices // 8) * 8
         self.count = 2 * (slices - 1) * slices
         self.LQ = -(-self.count // LANES) * LANES
 
@@ -82,15 +83,15 @@
 
 def kernel(
     plan, start_hbm, strain_hbm, fine_hbm, add_ref,
-    f, st, o, bx, ix, prod, mbuf,
-    in_sem, out_sem, halo_send, halo_recv, b_send, b_recv, i_send, i_recv, m_send, m_recv,
+    f, st, o, lo, hi, eb, bx, ix, prod, mz, mt,
+    in_sem, out_sem, halo_send, halo_recv, e_send, e_recv,
+    b_send, b_recv, i_send, i_recv, m_send, m_recv,
 ):
-    S, Z, C, D, X, Y, H, W, N = (
-        plan.S, plan.Z, plan.C, plan.D, plan.X, plan.Y, plan.H, plan.W, plan.N
+    S, Z, C, D, X, Y, H, R = (
+        plan.S, plan.Z, plan.C, plan.D, plan.X, plan.Y, plan.H, plan.R
     )
     p, rows, groups, rp, ny = plan.p, plan.rows, plan.groups, plan.rp, plan.ny
     t, s = lax.axis_index("tm"), lax.axis_index("space")
-    me = s * S + t
 
     load_start = pltpu.make_async_copy(start_hbm.at[0], f.at[:, pl.ds(2, D)], in_sem.at[0])
     load_start.start()
@@ -99,14 +100,32 @@
 
     barrier = pltpu.get_barrier_semaphore()
 
-    def greet(k, carry):
-        peer = lax.rem(me + k, N)
-        pl.semaphore_signal(
-            barrier, inc=1, device_id=(lax.rem(peer, S), peer // S), device_id_type=MESH
-        )
+    def greet_slices(slab, first):
+        def one(k, carry):
+            pl.semaphore_signal(
+                barrier, inc=1, device_id=(lax.rem(t + k, S), slab), device_id_type=MESH
+            )
+            return carry
+
+        lax.fori_loop(first, S, one, 0)
+
+    def greet_slab(slab, carry):
+        near = (slab - s <= H) & (s - slab <= H)
+
+        @pl.when(near & (slab != s))
+        def _():
+            greet_slices(slab, 0)
+
+        @pl.when(jnp.logical_not(near))
+        def _():
+            pl.semaphore_signal(barrier, inc=1, device_id=(t, slab), device_id_type=MESH)
+
         return carry
 
-    lax.fori_loop(1, N, greet, 0)
+    greet_slices(s, 1)
+    lax.fori_loop(0, Z, greet_slab, 0)
+    near_slabs = jnp.minimum(s + H, Z - 1) - jnp.maximum(s - H, 0) + 1
+    greetings = near_slabs * S - 1 + Z - near_slabs
 
     spread_y = pick(iota((Y, LANES), 0) // COARSEN == iota((Y, LANES), 1) % ny)
     tall = (groups * rows, p * X)
@@ -118,7 +137,7 @@
     def restrict(plane_sums):
         wide = dot(jnp.concatenate(plane_sums, axis=0), spread_y)
         result = []
-        for c in range(C):
+        for c in range(len(plane_sums)):
             tallc = dot(gather_x, wide[c * p * X : (c + 1) * p * X])
             total = jnp.zeros((rows, LANES), jnp.float32)
             for g in range(groups):
@@ -137,9 +156,16 @@
                 acc = acc + f[c, base + k]
             planes.append(acc)
         sums.append(jnp.concatenate(planes, axis=0))
-    own_b = restrict(sums)
+    for c in range(C):
+        bottom = (NEAR + FAR) * f[c, 2] + FAR * f[c, 3]
+        top = (NEAR + FAR) * f[c, D + 1] + FAR * f[c, D]
+        middle = [jnp.zeros((X, Y), jnp.float32)] * (p - 2)
+        sums.append(jnp.concatenate([bottom] + middle + [top], axis=0))
+    both = restrict(sums)
+    own_b, own_e = both[:C], both[C:]
     for c in range(C):
         bx[H, t, c] = own_b[c]
+        eb[0, c] = own_e[c]
 
     for d in range(-H, H + 1):
         if d != 0:
@@ -149,71 +175,78 @@
                 bx[H + d] = jnp.zeros((S, C, rows, LANES), jnp.float32)
                 ix[H + d] = jnp.zeros((S, C, rows, LANES), jnp.float32)
 
+    f[:, 0:2] = jnp.zeros((C, 2, X, Y), jnp.float32)
+    f[:, D + 2 : D + 4] = jnp.zeros((C, 2, X, Y), jnp.float32)
+
     @pl.when(s == 0)
     def _():
-        f[:, 0:2] = jnp.zeros((C, 2, X, Y), jnp.float32)
+        lo[...] = jnp.zeros((C, 2, X, Y), jnp.float32)
+        eb[1] = jnp.zeros((C, rows, LANES), jnp.float32)
 
     @pl.when(s == Z - 1)
     def _():
-        f[:, D + 2 : D + 4] = jnp.zeros((C, 2, X, Y), jnp.float32)
-
-    pl.semaphore_wait(barrier, N - 1)
-
-    up_copy = pltpu.make_async_remote_copy(
-        src_ref=f.at[:, pl.ds(D, 2)], dst_ref=f.at[:, pl.ds(0, 2)],
-        send_sem=halo_send.at[0], recv_sem=halo_recv.at[0],
-        device_id=(t, jnp.minimum(s + 1, Z - 1)), device_id_type=MESH,
-    )
-    down_copy = pltpu.make_async_remote_copy(
-        src_ref=f.at[:, pl.ds(2, 2)], dst_ref=f.at[:, pl.ds(D + 2, 2)],
-        send_sem=halo_send.at[1], recv_sem=halo_recv.at[1],
-        device_id=(t, jnp.maximum(s - 1, 0)), device_id_type=MESH,
-    )
-
-    def share(buf, send, recv):
-        order = sorted(range(-H, H + 1), key=abs)
+        hi[...] = jnp.zeros((C, 2, X, Y), jnp.float32)
+        eb[2] = jnp.zeros((C, rows, LANES), jnp.float32)
+
+    pl.semaphore_wait(barrier, greetings)
+
+    above, below = (t, jnp.minimum(s + 1, Z - 1)), (t, jnp.maximum(s - 1, 0))
+
+    def send(src, dst, send_sem, recv_sem, device):
+        return pltpu.make_async_remote_copy(
+            src_ref=src, dst_ref=dst, send_sem=send_sem, recv_sem=recv_sem,
+            device_id=device, device_id_type=MESH,
+        )
+
+    halo_up = send(f.at[:, pl.ds(D, 2)], lo, halo_send.at[0], halo_recv.at[0], above)
+    halo_down = send(f.at[:, pl.ds(2, 2)], hi, halo_send.at[1], halo_recv.at[1], below)
+    edge_up = send(eb.at[0], eb.at[1], e_send.at[0], e_recv.at[0], above)
+    edge_down = send(eb.at[0], eb.at[2], e_send.at[1], e_recv.at[1], below)
+
+    def at_up(*actions):
+        @pl.when(s < Z - 1)
+        def _():
+            for action in actions:
+                action()
+
+    def at_down(*actions):
+        @pl.when(s > 0)
+        def _():
+            for action in actions:
+                action()
+
+    near_order = sorted(range(-R, R + 1), key=abs)
+    far_order = [d for d in range(-H, H + 1) if abs(d) > R]
+
+    def share(buf, send_sem, recv_sem, order, condition=True):
         for d in order:
 
             def one(k, carry):
-                pltpu.make_async_remote_copy(
-                    src_ref=buf.at[H, t], dst_ref=buf.at[H - d, t],
-                    send_sem=send.at[H + d], recv_sem=recv.at[H - d],
-                    device_id=(lax.rem(t + k, S), s + d), device_id_type=MESH,
+                send(
+                    buf.at[H, t], buf.at[H - d, t], send_sem.at[H + d], recv_sem.at[H - d],
+                    (lax.rem(t + k, S), s + d),
                 ).start()
                 return carry
 
-            @pl.when((s + d >= 0) & (s + d < Z))
+            @pl.when((s + d >= 0) & (s + d < Z) & condition)
             def _():
                 lax.fori_loop(1 if d == 0 else 0, S, one, 0)
 
-    def settle(buf, sem):
-        for d in range(-H, H + 1):
-            size = S - 1 if d == 0 else S
-
-            @pl.when((s + d >= 0) & (s + d < Z))
+    def settle(buf, sem, order, size=S, condition=True):
+        for d in order:
+
+            @pl.when((s + d >= 0) & (s + d < Z) & condition)
             def _():
-                view = buf.at[H + d, pl.ds(0, size)]
+                view = buf.at[H + d, pl.ds(0, size - 1 if d == 0 else size)]
                 pltpu.make_async_copy(view, view, sem.at[H + d]).wait()
 
-    share(bx, b_send, b_recv)
-
-    @pl.when(s < Z - 1)
-    def _():
-        up_copy.start()
-
-    @pl.when(s > 0)
-    def _():
-        down_copy.start()
-
+    at_up(edge_up.start)
+    at_down(edge_down.start)
+    share(bx, b_send, b_recv, near_order)
+    at_up(halo_up.start)
+    at_down(halo_down.start)
+    share(bx, b_send, b_recv, far_order)
     load_strain.wait()
-
-    @pl.when(s > 0)
-    def _():
-        up_copy.wait_recv()
-
-    @pl.when(s < Z - 1)
-    def _():
-        down_copy.wait_recv()
 
     near, far = DIFFUSION * NEAR, DIFFUSION * FAR
     centre = 1.0 - 6.0 * (near + far)
@@ -230,29 +263,32 @@
             acc = centre * v[c] + near * n1 + far * n2
             for j in range(C):
                 acc += st[C * c + j, z].astype(jnp.float32) * v[j]
-            o[c, z] = acc
+            o[c, z // COARSEN, z % COARSEN] = acc
         return carry
 
     lax.fori_loop(0, D, fine_plane, 0)
-    store_fine = pltpu.make_async_copy(o, fine_hbm, out_sem)
-    store_fine.start()
-
     sums = []
     for c in range(C):
         planes = []
         for zz in range(p):
-            acc = o[c, zz * COARSEN]
+            acc = o[c, zz, 0]
             for k in range(1, COARSEN):
-                acc = acc + o[c, zz * COARSEN + k]
+                acc = acc + o[c, zz, k]
             planes.append(acc)
         sums.append(jnp.concatenate(planes, axis=0))
     own_i = restrict(sums)
-    for c in range(C):
+    tools = step_tools(plan)
+    at_down(edge_up.wait_recv)
+    at_up(edge_down.wait_recv)
+    for c in range(C):
+        edge = jnp.where(tools["first_z"], pltpu.roll(eb[1, c], rp, 0), 0.0)
+        edge += jnp.where(tools["last_z"], pltpu.roll(eb[2, c], rows - rp, 0), 0.0)
+        own_i[c] = own_i[c] + DIFFUSION * edge
         ix[H, t, c] = own_i[c]
-    share(ix, i_send, i_recv)
-
-    settle(bx, b_recv)
-    tools = step_tools(plan)
+    share(ix, i_send, i_recv, near_order)
+    share(ix, i_send, i_recv, far_order, t == 0)
+
+    settle(bx, b_recv, near_order)
     inside = [(s + d >= 0) & (s + d < Z) for d in range(-H, H + 1)]
 
     def advance(m_fields, reach):
@@ -287,21 +323,24 @@
     else:
         lax.fori_loop(0, S, powers, 0)
     message = dot(jnp.ones((8, LANES), jnp.float32), prod[:, 0, :], ((1,), (1,)))
-    mbuf[me] = message[0:1]
-
-    def tell(k, carry):
-        peer = lax.rem(me + k, N)
-        pltpu.make_async_remote_copy(
-            src_ref=mbuf.at[me], dst_ref=mbuf.at[me], send_sem=m_send, recv_sem=m_recv,
-            device_id=(lax.rem(peer, S), peer // S), device_id_type=MESH,
-        ).start()
-        return carry
-
-    lax.fori_loop(1, N, tell, 0)
-    view = mbuf.at[pl.ds(0, N - 1)]
-    pltpu.make_async_copy(view, view, m_recv).wait()
-    owner = pick(iota((N, LANES), 0) % S == iota((N, LANES), 1))
-    table = dot(mbuf[:, 0, :], owner, ((0,), (0,)))
+    def tell(buf, index, size, step, device):
+        def one(k, carry):
+            send(buf.at[index], buf.at[index], m_send.at[step], m_recv.at[step], device(k)).start()
+            return carry
+
+        lax.fori_loop(1, size, one, 0)
+        view = buf.at[pl.ds(0, size - 1)]
+        pltpu.make_async_copy(view, view, m_recv.at[step]).wait()
+        return pltpu.make_async_copy(view, view, m_send.at[step])
+
+    mz[s] = message[0:1]
+    if plan.SP > S:
+        mt[pl.ds(S, plan.SP - S)] = jnp.zeros((plan.SP - S, 1, plan.LQ), jnp.float32)
+    told_z = tell(mz, s, Z, 0, lambda k: (t, lax.rem(s + k, Z)))
+    mt[t] = jnp.sum(mz[:, 0, :], axis=0, keepdims=True)
+    told_t = tell(mt, t, S, 1, lambda k: (lax.rem(t + k, S), s))
+    owner = pick(iota((plan.SP, LANES), 0) == iota((plan.SP, LANES), 1))
+    table = dot(mt[:, 0, :], owner, ((0,), (0,)))
 
     def block(kind, k):
         at = (kind * (S - 1) + k) * S
@@ -333,7 +372,18 @@
             jnp.where(lane1 < S, jnp.sum(inverse * p_col, axis=0, keepdims=True), 0.0)
         )
 
-    settle(ix, i_recv)
+    at_down(halo_up.wait_recv)
+    at_up(halo_down.wait_recv)
+    for c in range(C):
+        o[c, 0, 0] += far * lo[c, 0] + near * lo[c, 1]
+        o[c, 0, 1] += far * lo[c, 1]
+        o[c, p - 1, COARSEN - 1] += near * hi[c, 0] + far * hi[c, 1]
+        o[c, p - 1, COARSEN - 2] += far * hi[c, 0]
+    store_fine = pltpu.make_async_copy(o, fine_hbm, out_sem)
+    store_fine.start()
+    settle(bx, b_recv, far_order)
+    settle(ix, i_recv, near_order)
+    settle(ix, i_recv, far_order, 1)
 
     carried = []
     weights = [
@@ -374,17 +424,13 @@
             add_ref[c, zz] = full[zz * X : (zz + 1) * X]
 
     store_fine.wait()
-    settle(bx, b_send)
-    settle(ix, i_send)
-    pltpu.make_async_copy(view, view, m_send).wait()
-
-    @pl.when(s < Z - 1)
-    def _():
-        up_copy.wait_send()
-
-    @pl.when(s > 0)
-    def _():
-        down_copy.wait_send()
+    settle(bx, b_send, near_order + far_order)
+    settle(ix, i_send, near_order)
+    settle(ix, i_send, far_order, S, t == 0)
+    told_z.wait()
+    told_t.wait()
+    at_up(halo_up.wait_send, edge_up.wait_send)
+    at_down(halo_down.wait_send, edge_down.wait_send)
 
 
 def local(starts, strain):
@@ -397,7 +443,7 @@
     fine, add = pl.pallas_call(
         functools.partial(kernel, plan),
         out_shape=(
-            jax.ShapeDtypeStruct((C, D, X, Y), f32),
+            jax.ShapeDtypeStruct((C, plan.p, COARSEN, X, Y), f32),
             jax.ShapeDtypeStruct((C, plan.p, X, Y), f32),
         ),
         in_specs=[pl.BlockSpec(memory_space=pl.ANY)] * 2,
@@ -408,19 +454,22 @@
         scratch_shapes=[
             pltpu.VMEM((C, D + 4, X, Y), f32),
             pltpu.VMEM(strain.shape[1:], strain.dtype),
-            pltpu.VMEM((C, D, X, Y), f32),
+            pltpu.VMEM((C, plan.p, COARSEN, X, Y), f32),
+            pltpu.VMEM((C, 2, X, Y), f32),
+            pltpu.VMEM((C, 2, X, Y), f32),
+            pltpu.VMEM((3, C, plan.rows, LANES), f32),
             pltpu.VMEM(coarse, f32),
             pltpu.VMEM(coarse, f32),
             pltpu.VMEM((plan.LQ, 1, LANES), f32),
-            pltpu.VMEM((plan.N, 1, plan.LQ), f32),
-            dma((2,)), dma(()), dma((2,)), dma((2,)),
+            pltpu.VMEM((slabs, 1, plan.LQ), f32),
+            pltpu.VMEM((plan.SP, 1, plan.LQ), f32),
+            dma((2,)), dma(()), dma((2,)), dma((2,)), dma((2,)), dma((2,)),
             dma((plan.W,)), dma((plan.W,)), dma((plan.W,)), dma((plan.W,)),
-            dma(()), dma(()),
+            dma((2,)), dma((2,)),
         ],
         compiler_params=pltpu.CompilerParams(collective_id=0, has_side_effects=True),
     )(starts, strain)
-    shape = (C, plan.p, COARSEN, X, Y)
-    return (fine.reshape(shape) + add[:, :, None]).reshape(1, C, D, X, Y)
+    return (fine + add[:, :, None]).reshape(1, C, D, X, Y)
 
 
 def solution(mesh):

time: 24.6 us -> 23 us (0.935)
  Pallas kernels: 22.2 us -> 20.6 us
  local copies, waits for them, and re-layouts: 1.21 us -> 0 us
  other arithmetic: 1 us -> 2.14 us
    pallas_call x1, Pallas kernels: 22.2 us -> 20.6 us  [local(): pl.pallas_call(functools.partial(kernel, plan), out_shape=(jax.ShapeDtype...]
    add x1, other arithmetic: 1 us -> 2.14 us  [local(): return (fine + add[:, :, None]).reshape(1, C, D, X, Y)]
    add x1 -> x0, local copies, waits for them, and re-layouts: 1.07 us -> none  [local(): return (fine.reshape(shape) + add[:, :, None]).reshape(1, C, D, X, Y)]
where the time goes in v2:
time: 23 us; the launch traced here: 22.8 us
  Pallas kernels  20.6 us (90%)
  other arithmetic  2.14 us (9%)
    pallas_call x1, Pallas kernels, local(): pl.pallas_call(functools.partial(kernel, plan), out_shape=(jax.ShapeDtype...  20.6 us
    add x1, other arithmetic, local(): return (fine + add[:, :, None]).reshape(1, C, D, X, Y)  2.14 us

profile of v2, /device:TPU:0, one launch (start us, length us, event | category | flops | bytes accessed | tf_op | source)
XLA Modules:
  0.0 22.8 jit_solution(14679445184118744495)
XLA Ops:
  0.0 20.6 %shard_map.28 = (f32[3,2,4,64,128]{4,3,2,1,0:T(8,128)}, f32[3,2,64,128]{3,2,1,0:T(8,128)}) custom-call(f32[1,3,8,64,128]{4,3,2,1,0:T(8,128)} %start_hbm.1, bf16[1,9,8,64,128]{4,3,2,1,0:T(8,128)(2,1)} %strain_hbm.1), custom_call_target="tpu_custom_call" | custom-call | tf_op jit(solution)/shard_map/pallas_call | solution.py:443
  20.7 2.1 %broadcast_add_fusion = f32[3,2,4,64,128]{4,3,2,1,0:T(8,128)} fusion(f32[3,2,4,64,128]{4,3,2,1,0:T(8,128)} %get-tuple-element.7, f32[3,2,64,128]{3,2,1,0:T(8,128)} %get-tuple-element.8), kind=kLoop, calls=%fused_computation | loop fusion | flops 196608 | bytes 1769472 | tf_op jit(solution)/shard_map/add | solution.py:472

commit v3 on v2

--- a/solution.py
+++ b/solution.py
@@ -82,9 +82,9 @@
 
 
 def kernel(
-    plan, start_hbm, strain_hbm, fine_hbm, add_ref,
-    f, st, o, lo, hi, eb, bx, ix, prod, mz, mt,
-    in_sem, out_sem, halo_send, halo_recv, e_send, e_recv,
+    plan, start_hbm, strain_hbm, o,
+    f, st, lo, hi, eb, bx, ix, prod, mz, mt,
+    in_sem, halo_send, halo_recv, e_send, e_recv,
     b_send, b_recv, i_send, i_recv, m_send, m_recv,
 ):
     S, Z, C, D, X, Y, H, R = (
@@ -245,7 +245,6 @@
     share(bx, b_send, b_recv, near_order)
     at_up(halo_up.start)
     at_down(halo_down.start)
-    share(bx, b_send, b_recv, far_order)
     load_strain.wait()
 
     near, far = DIFFUSION * NEAR, DIFFUSION * FAR
@@ -285,8 +284,6 @@
         edge += jnp.where(tools["last_z"], pltpu.roll(eb[2, c], rows - rp, 0), 0.0)
         own_i[c] = own_i[c] + DIFFUSION * edge
         ix[H, t, c] = own_i[c]
-    share(ix, i_send, i_recv, near_order)
-    share(ix, i_send, i_recv, far_order, t == 0)
 
     settle(bx, b_recv, near_order)
     inside = [(s + d >= 0) & (s + d < Z) for d in range(-H, H + 1)]
@@ -323,12 +320,13 @@
     else:
         lax.fori_loop(0, S, powers, 0)
     message = dot(jnp.ones((8, LANES), jnp.float32), prod[:, 0, :], ((1,), (1,)))
-    def tell(buf, index, size, step, device):
+    def tell(buf, index, size, step, device, meanwhile=lambda: None):
         def one(k, carry):
             send(buf.at[index], buf.at[index], m_send.at[step], m_recv.at[step], device(k)).start()
             return carry
 
         lax.fori_loop(1, size, one, 0)
+        meanwhile()
         view = buf.at[pl.ds(0, size - 1)]
         pltpu.make_async_copy(view, view, m_recv.at[step]).wait()
         return pltpu.make_async_copy(view, view, m_send.at[step])
@@ -336,7 +334,13 @@
     mz[s] = message[0:1]
     if plan.SP > S:
         mt[pl.ds(S, plan.SP - S)] = jnp.zeros((plan.SP - S, 1, plan.LQ), jnp.float32)
-    told_z = tell(mz, s, Z, 0, lambda k: (t, lax.rem(s + k, Z)))
+
+    def bulk():
+        share(bx, b_send, b_recv, far_order)
+        share(ix, i_send, i_recv, near_order)
+        share(ix, i_send, i_recv, far_order, t == 0)
+
+    told_z = tell(mz, s, Z, 0, lambda k: (t, lax.rem(s + k, Z)), bulk)
     mt[t] = jnp.sum(mz[:, 0, :], axis=0, keepdims=True)
     told_t = tell(mt, t, S, 1, lambda k: (lax.rem(t + k, S), s))
     owner = pick(iota((plan.SP, LANES), 0) == iota((plan.SP, LANES), 1))
@@ -379,8 +383,6 @@
         o[c, 0, 1] += far * lo[c, 1]
         o[c, p - 1, COARSEN - 1] += near * hi[c, 0] + far * hi[c, 1]
         o[c, p - 1, COARSEN - 2] += far * hi[c, 0]
-    store_fine = pltpu.make_async_copy(o, fine_hbm, out_sem)
-    store_fine.start()
     settle(bx, b_recv, far_order)
     settle(ix, i_recv, near_order)
     settle(ix, i_recv, far_order, 1)
@@ -421,9 +423,8 @@
         tallc = dot(gather_x, stack, ((0,), (0,)))
         full = dot(tallc, spread_y, ((1,), (1,)))
         for zz in range(p):
-            add_ref[c, zz] = full[zz * X : (zz + 1) * X]
-
-    store_fine.wait()
+            for k in range(COARSEN):
+                o[c, zz, k] += full[zz * X : (zz + 1) * X]
     settle(bx, b_send, near_order + far_order)
     settle(ix, i_send, near_order)
     settle(ix, i_send, far_order, S, t == 0)
@@ -440,21 +441,14 @@
     f32 = jnp.float32
     coarse = (plan.W, plan.S, C, plan.rows, LANES)
     dma = pltpu.SemaphoreType.DMA
-    fine, add = pl.pallas_call(
+    corrected = pl.pallas_call(
         functools.partial(kernel, plan),
-        out_shape=(
-            jax.ShapeDtypeStruct((C, plan.p, COARSEN, X, Y), f32),
-            jax.ShapeDtypeStruct((C, plan.p, X, Y), f32),
-        ),
+        out_shape=pltpu.VMEM((C, plan.p, COARSEN, X, Y), f32),
         in_specs=[pl.BlockSpec(memory_space=pl.ANY)] * 2,
-        out_specs=(
-            pl.BlockSpec(memory_space=pl.ANY),
-            pl.BlockSpec(memory_space=pltpu.VMEM),
-        ),
+        out_specs=pl.BlockSpec(memory_space=pltpu.VMEM),
         scratch_shapes=[
             pltpu.VMEM((C, D + 4, X, Y), f32),
             pltpu.VMEM(strain.shape[1:], strain.dtype),
-            pltpu.VMEM((C, plan.p, COARSEN, X, Y), f32),
             pltpu.VMEM((C, 2, X, Y), f32),
             pltpu.VMEM((C, 2, X, Y), f32),
             pltpu.VMEM((3, C, plan.rows, LANES), f32),
@@ -463,13 +457,13 @@
             pltpu.VMEM((plan.LQ, 1, LANES), f32),
             pltpu.VMEM((slabs, 1, plan.LQ), f32),
             pltpu.VMEM((plan.SP, 1, plan.LQ), f32),
-            dma((2,)), dma(()), dma((2,)), dma((2,)), dma((2,)), dma((2,)),
+            dma((2,)), dma((2,)), dma((2,)), dma((2,)), dma((2,)),
             dma((plan.W,)), dma((plan.W,)), dma((plan.W,)), dma((plan.W,)),
             dma((2,)), dma((2,)),
         ],
         compiler_params=pltpu.CompilerParams(collective_id=0, has_side_effects=True),
     )(starts, strain)
-    return (fine + add[:, :, None]).reshape(1, C, D, X, Y)
+    return corrected.reshape(1, C, D, X, Y)
 
 
 def solution(mesh):

time: 23 us -> 20.7 us (0.900)
  other arithmetic: 2.14 us -> 0 us
  Pallas kernels: 20.6 us -> 19.6 us
  local copies, waits for them, and re-layouts: 0 us -> 0.88 us
    add x1 -> x0, other arithmetic: 2.14 us -> none  [local(): return (fine + add[:, :, None]).reshape(1, C, D, X, Y)]
    pallas_call x1, Pallas kernels: 20.6 us -> 19.6 us  [local(): pl.pallas_call(functools.partial(kernel, plan), out_shape=pltpu.VMEM((C,...]
    unnamed x0 -> x1, local copies, waits for them, and re-layouts: none -> 0.88 us
where the time goes in v3:
time: 20.7 us; the launch traced here: 20.5 us
  Pallas kernels  19.6 us (95%)
  local copies, waits for them, and re-layouts  0.88 us (4%)
    pallas_call x1, Pallas kernels, local(): pl.pallas_call(functools.partial(kernel, plan), out_shape=pltpu.VMEM((C,...  19.6 us
    unnamed x1, local copies, waits for them, and re-layouts  0.88 us

profile of v3, /device:TPU:0, one launch (start us, length us, event | category | flops | bytes accessed | tf_op | source)
XLA Modules:
  0.0 20.5 jit_solution(9591521356238459210)
XLA Ops:
  0.0 19.6 %shard_map.28 = f32[3,2,4,64,128]{4,3,2,1,0:T(8,128)S(1)} custom-call(f32[1,3,8,64,128]{4,3,2,1,0:T(8,128)} %start_hbm.1, bf16[1,9,8,64,128]{4,3,2,1,0:T(8,128)(2,1)} %strain_hbm.1), custom_call_target="tpu_custom_call" | custom-call | tf_op jit(solution)/shard_map/pallas_call | solution.py:444
  19.6 0.9 %copy.4 = f32[1,3,8,64,128]{4,3,2,1,0:T(8,128)} copy(f32[1,3,8,64,128]{4,3,2,1,0:T(8,128)S(1)} %bitcast.1) | data formatting | bytes 1572864
